TPU v7x, 256 devices: a whole 4x4x8 slice. The times are simulated.
256 devices in a mesh: frame: 16 (over x, z_lo), fsdp: 16 (over z_hi, y, core).
Axes of the slice: x: 4, y: 4, z: 8 (z_hi: 2, z_lo: 4; z = z_hi * 4 + z_lo), core: 2. Of those that a mesh axis runs over, the one named last changes fastest.
Arguments:
- queries: bfloat16 [256, 192, 3072], P(('frame', 'fsdp')), may hold values from -18 to 18
- keys: bfloat16 [256, 192, 3072], P(('frame', 'fsdp')), may hold values from -7 to 7
- values: bfloat16 [256, 192, 3072], P(('frame', 'fsdp')), may hold values from -6 to 6
- residual: bfloat16 [256, 192, 3072], P(('frame', 'fsdp')), may hold values from -6 to 6
- target: bfloat16 [256, 192, 3072], P(('frame', 'fsdp')), may hold values from -6 to 6
- output_weight: bfloat16 [3072, 3072], P('fsdp'), may hold values from -0.109375 to 0.109375
- down_adapter: bfloat16 [16, 64, 3072], P('frame', None, 'fsdp'), may hold values from -0.109375 to 0.109375
- up_adapter: bfloat16 [16, 64, 3072], P('frame', None, 'fsdp'), may hold values from -1.1953125 to 1.1953125
- scene_of_frame: int32 [256], P(('frame', 'fsdp')), may hold values from 0 to 15
- scene_adapter_row: int32 [16], replicated, may hold values from 0 to 15, each once
- valid_token_count: int32 [256], P(('frame', 'fsdp')), may hold values from 1 to 192, 30720 in all
Outputs:
- grad_down: float32 [16, 64, 3072], P('frame', None, 'fsdp')
- grad_up: float32 [16, 64, 3072], P('frame', None, 'fsdp')
- frame_loss: float32 [256], P(('frame', 'fsdp'))
Inputs may be any that keep to these rules, and one draw needn't show every extreme that they name: `scene_adapter_row`: each scene has its own adapter row. `valid_token_count`: some frame has all 192 slots valid.
All inputs are finite; a program needn't handle non-finite values. No bound on the sum of `valid_token_count` on one device may be relied on, other than what follows from the above.
Results may differ from a plain program's by a relative error of at most 0.0053.
Values may be sent and summed in bfloat16 or wider, within the bound.
A program may use at most 192 MiB of HBM per device.

v0:
```python
import math
import jax
import jax.numpy as jnp
from jax import lax
from jax.sharding import PartitionSpec as P

HEADS = 24
adapter_scale = 2.0


def slot_lookup(scene_ids, scene_adapter_row):
    scene_range = jnp.arange(scene_adapter_row.shape[0], dtype=jnp.int32)
    matches = scene_ids[:, None] == scene_range[None, :]
    return jnp.sum(jnp.where(matches, scene_adapter_row[None, :], 0), axis=1)


def per_device(
    queries,
    keys,
    values,
    residual,
    target,
    output_weight,
    down_adapter,
    up_adapter,
    scene_of_frame,
    scene_adapter_row,
    valid_token_count,
):
    frames, slot_count, model_width = queries.shape
    head_count = HEADS
    head_size = model_width // head_count
    row_count = frames * slot_count
    score_scale = 1.0 / math.sqrt(head_size)
    query_heads = queries.reshape(frames, slot_count, head_count, head_size)
    key_heads = keys.reshape(frames, slot_count, head_count, head_size)
    value_heads = values.reshape(frames, slot_count, head_count, head_size)
    scores = (
        jnp.einsum("fqhd,fkhd->fhqk", query_heads, key_heads, preferred_element_type=jnp.float32)
        * score_scale
    )
    positions = lax.broadcasted_iota(jnp.int32, (frames, slot_count), 1)
    valid_mask = positions < valid_token_count[:, None]
    scores = jnp.where(valid_mask[:, None, None, :], scores, -jnp.inf)
    row_max = jnp.max(scores, axis=-1, keepdims=True)
    exponent = jnp.exp(scores - row_max)
    weights = (exponent / jnp.sum(exponent, axis=-1, keepdims=True)).astype(jnp.bfloat16)
    attended = jnp.einsum(
        "fhqk,fkhd->fqhd", weights, value_heads, preferred_element_type=jnp.float32
    )
    attended = attended.astype(jnp.bfloat16).reshape(frames, slot_count, model_width)
    mixed_flat = attended.reshape(row_count, model_width)
    projected_tokens = jnp.dot(
        mixed_flat,
        lax.all_gather(output_weight, "fsdp", axis=0, tiled=True),
        preferred_element_type=jnp.float32,
    )
    projected_tokens = projected_tokens.reshape(frames, slot_count, model_width)
    column_ids = lax.all_gather(scene_of_frame, "fsdp", axis=0, tiled=True)
    column_slots = slot_lookup(column_ids, scene_adapter_row)
    owner_range = jnp.arange(scene_adapter_row.shape[0], dtype=jnp.int32)
    column_pick = column_slots[:, None] == owner_range[None, :]
    adapter_couple = jnp.stack([down_adapter, up_adapter], axis=1)
    blocks = lax.all_gather(adapter_couple, "frame", axis=0, tiled=True)
    chosen = jnp.einsum(
        "fs,sxrd->fxrd",
        column_pick.astype(jnp.bfloat16),
        blocks,
        preferred_element_type=jnp.float32,
    )
    adapters = lax.all_to_all(
        chosen.astype(jnp.bfloat16), "fsdp", split_axis=0, concat_axis=3, tiled=True
    )
    down_weight_rows = adapters[:, 0]
    up_weight_rows = adapters[:, 1]
    low_rank_state = jnp.einsum(
        "ftd,frd->ftr", attended, down_weight_rows, preferred_element_type=jnp.float32
    ).astype(jnp.bfloat16)
    adapter_output = jnp.einsum(
        "akw,awe->ake", low_rank_state, up_weight_rows, preferred_element_type=jnp.float32
    )
    combined_output = (
        residual.astype(jnp.float32)
        + projected_tokens
        + adapter_scale * adapter_output
        - target.astype(jnp.float32)
    )
    residual_error = jnp.where(
        valid_mask[:, :, None], combined_output, jnp.zeros_like(combined_output)
    )
    token_float = valid_token_count.astype(jnp.float32)
    frame_loss = jnp.sum(residual_error * residual_error, axis=(1, 2)) / (token_float * model_width)
    output_gradient = (2.0 * residual_error / token_float[:, None, None]).astype(jnp.bfloat16)
    up_gradient_terms = adapter_scale * jnp.einsum(
        "ftr,ftd->frd", low_rank_state, output_gradient, preferred_element_type=jnp.float32
    )
    backward_low_rank = (
        adapter_scale
        * jnp.einsum(
            "ftd,frd->ftr", output_gradient, up_weight_rows, preferred_element_type=jnp.float32
        )
    ).astype(jnp.bfloat16)
    down_terms = jnp.einsum(
        "ftr,ftd->frd", backward_low_rank, attended, preferred_element_type=jnp.float32
    )
    grad_terms = jnp.stack([down_terms, up_gradient_terms], axis=1)
    pieces = lax.all_to_all(grad_terms, "fsdp", split_axis=3, concat_axis=0, tiled=True)
    scene_dense = jnp.einsum(
        "fs,fxrd->sxrd", column_pick.astype(jnp.float32), pieces, precision=lax.Precision.HIGHEST
    )
    scene_full = lax.psum(scene_dense, "frame")
    owned_rows = lax.dynamic_slice_in_dim(scene_full, lax.axis_index("frame"), 1, 0)
    return (owned_rows[:, 0], owned_rows[:, 1], frame_loss)


def solution(mesh):
    placed = (
        P(("frame", "fsdp"), None, None),
        P(("frame", "fsdp"), None, None),
        P(("frame", "fsdp"), None, None),
        P(("frame", "fsdp"), None, None),
        P(("frame", "fsdp"), None, None),
        P("fsdp", None),
        P("frame", None, "fsdp"),
        P("frame", None, "fsdp"),
        P(("frame", "fsdp")),
        P(),
        P(("frame", "fsdp")),
    )
    return jax.shard_map(
        per_device,
        mesh=mesh,
        in_specs=placed,
        out_specs=(P("frame", None, "fsdp"), P("frame", None, "fsdp"), P(("frame", "fsdp"))),
        check_vma=False,
    )
```

profile of v0, /device:TPU:16, one launch (start us, length us, event | category | flops | bytes accessed | tf_op | source)
XLA Modules:
  0.0 509.0 jit_solution(2743683499181057483)
XLA Ops:
  7.2 0.0 all-gather.2.cloned.1.call-start
  7.2 0.7 all-gather.2.cloned.1.call-update
  8.6 1.3 dynamic-slice
  9.8 0.8 dynamic-update-slice
  10.6 15.7 %all-reduce = s32[16]{0:T(128)S(1)} all-reduce(s32[16]{0:T(128)S(1)} %dynamic-update-slice), channel_id=1, replica_groups=mesh['frame'=16,'fsdp'=16] {'fsdp'}, use_global_device_ids=true, to_apply=%add | all-reduce | flops 16 | bytes 128
  26.3 0.8 select_reduce_fusion
  27.1 0.8 pad_maximum_fusion.1
  27.9 76.0 %all_gather.11 = bf16[16,2,64,192]{3,2,1,0:T(8,128)(2,1)S(1)} all-gather(bf16[1,2,64,192]{3,2,1,0:T(8,128)(2,1)S(1)} %pad_maximum_fusion.1), channel_id=1, replica_groups=mesh['frame'=16,'fsdp'=16] {'frame'}, dimensions={0}, use_global_device_ids=true | all-gather | bytes 835584 | tf_op jit(solution)/shard_map/all_gather | solution.py:64
  103.9 0.7 convolution_convert_fusion
  104.6 0.0 copy-start
  104.6 1.3 copy.63
  106.0 4.8 all-to-all-start
  110.8 0.0 all-reduce.3.cloned.1.call-start
  111.5 0.0 copy-done
  111.5 0.0 copy-start.1
  111.5 0.2 copy.74
  111.7 1.6 copy.75
  113.3 0.0 copy-done.1
  113.3 0.2 copy.76
  113.6 0.8 fusion.24
  114.4 2.0 fusion.51
  116.3 1.1 fusion.15
  117.5 1.8 copy.60
  119.3 54.0 %all-to-all-done = bf16[16,2,64,192]{3,2,1,0:T(8,128)(2,1)S(1)} async-done(((bf16[16,2,64,192]{3,2,1,0:T(8,128)(2,1)}), bf16[16,2,64,192]{3,2,1,0:T(8,128)(2,1)S(1)}, u32[]{:S(2)}, u32[]{:S(2)}) %all-to-all-start) | async-done | bytes 786464 | tf_op jit(solution)/shard_map/all_to_all | solution.py:71
  173.3 0.6 copy.64
  173.9 0.0 copy-start.2
  173.9 1.1 all_to_all.29
  175.0 1.8 fusion.33
  176.8 58.8 %all-gather.2.cloned.1.call-done = bf16[3072,3072]{1,0:T(8,128)(2,1)} async-done(((bf16[192,3072]{1,0:T(8,128)(2,1)}), bf16[3072,3072]{1,0:T(8,128)(2,1)}) %all-gather.2.cloned.1.call-update) | async-done | bytes 18874384 | tf_op jit(solution)/shard_map/all_gather | solution.py:55
  235.6 0.0 copy-done.2
  235.6 0.0 copy-start.3
  235.6 9.1 %fusion.5 = f32[1,192,3072]{2,1,0:T(8,128)S(1)} fusion(bf16[3072,3072]{1,0:T(8,128)(2,1)} %all-gather.2.cloned.1.call-done, bf16[1,192,3072]{2,1,0:T(8,128)(2,1)} %param.14, bf16[24,8,24,128]{3,2,1,0:T(8,128)(2,1)S(1)} %bitcast.107), kind=kOutput, calls=%fused_computation.10 | convolution fusion | flops 3625058304 | bytes 23592960 | tf_op jit(solution)/shard_map/dot_general | solution.py:53
  244.7 0.0 copy-done.3
  244.7 1.5 multiply_reduce_fusion
  246.2 1.3 fusion.7
  247.4 3.2 convolution_bitcast_fusion.1
  250.6 2.7 pad_maximum_fusion
  253.3 4.4 copy.65
  257.8 4.2 reshape.120
  262.0 42.7 %all_to_all.36 = f32[16,1,24576]{2,1,0:T(1,128)S(1)} all-to-all(f32[16,1,24576]{2,1,0:T(1,128)} %reshape.120), channel_id=1, replica_groups=mesh['frame'=16,'fsdp'=16] {'fsdp'}, dimensions={0} | all-to-all | bytes 3145728 | tf_op jit(solution)/shard_map/all_to_all | solution.py:107
  304.7 0.5 broadcast.46
  305.2 6.0 %reduce.5 = f32[16,24576]{1,0:T(8,128)} reduce(f32[16,1,24576]{2,1,0:T(1,128)S(1)} %all_to_all.36, f32[]{:T(128)} %broadcast.46), dimensions={1}, to_apply=%all_to_all.30.reduce_sub_computation | reduce | bytes 3145732 | tf_op jit(solution)/shard_map/all_to_all | solution.py:107
  311.2 3.4 reshape.121
  314.7 3.8 copy.73
  318.5 4.0 fusion.12
  322.5 0.0 all-reduce.3.cloned.1.call-update
  323.2 175.3 %all-reduce.3.cloned.1.call-done = f32[16,2,64,192]{3,0,2,1:T(8,128)} async-done(((f32[16,2,64,192]{3,0,2,1:T(8,128)}), f32[16,2,64,192]{3,0,2,1:T(8,128)}) %all-reduce.3.cloned.1.call-update) | async-done | bytes 1572880 | tf_op jit(solution)/shard_map/psum | solution.py:111
  498.5 1.3 dynamic-slice_bitcast_fusion
  499.8 0.6 copy.67
  500.4 0.6 copy.68
  (2 shorter events, 0.0 us)
Async XLA Ops:
  7.2 228.4 %all-gather.2.cloned.1.call-start = ((), (), s32[]{:S(2)}) async-start(), calls=%async_computation.2 | async-start | bytes 20054016 | tf_op jit(solution)/shard_map/all_gather | solution.py:55
  104.6 6.9 %copy-start = (bf16[1,192,3072]{2,1,0:T(8,128)(2,1)S(1)}, bf16[1,192,3072]{2,1,0:T(8,128)(2,1)}, u32[]{:S(2)}) copy-start(bf16[1,192,3072]{2,1,0:T(8,128)(2,1)} %param.11) | copy-start | bytes 3538948
  106.0 67.3 %all-to-all-start = ((bf16[16,2,64,192]{3,2,1,0:T(8,128)(2,1)}), bf16[16,2,64,192]{3,2,1,0:T(8,128)(2,1)S(1)}, u32[]{:S(2)}, u32[]{:S(2)}) async-start(bf16[16,2,64,192]{3,2,1,0:T(8,128)(2,1)} %copy.63), calls=%async_computation | async-start | bytes 2097152 | tf_op jit(solution)/shard_map/all_to_all | solution.py:71
  110.8 387.7 %all-reduce.3.cloned.1.call-start = ((), (), s32[]{:S(2)}) async-start(), calls=%async_computation.3 | async-start | bytes 4194304 | tf_op jit(solution)/shard_map/psum | solution.py:111
  111.5 1.8 copy-start.1
  173.9 61.7 %copy-start.2 = (bf16[1,192,24,128]{3,2,1,0:T(8,128)(2,1)S(1)}, bf16[1,192,24,128]{3,2,1,0:T(8,128)(2,1)}, u32[]{:S(2)}) copy-start(bf16[1,192,24,128]{3,2,1,0:T(8,128)(2,1)} %copy.60) | copy-start | bytes 3538948
  235.6 9.1 %copy-start.3 = (bf16[1,192,3072]{2,1,0:T(8,128)(2,1)S(1)}, bf16[1,192,3072]{2,1,0:T(8,128)(2,1)}, u32[]{:S(2)}) copy-start(bf16[1,192,3072]{2,1,0:T(8,128)(2,1)} %param.15) | copy-start | bytes 3538948
Sparse Core Ops, SparseCore 0:
  10.7 224.8 all-gather.1
  322.6 175.7 all-reduce.2
where the time goes:
time: 510 us; the launch traced here: 509 us
  waiting for transfers between devices  289 us (57%)
  blocking collectives  134 us (26%)
  local copies, waits for them, and re-layouts  27.8 us (5%)
  matrix products  23.4 us (5%)
  between operations  17.3 us (3%)
  other arithmetic  12.3 us (2%)
    psum x1, waiting for transfers between devices, per_device(): scene_full = lax.psum(scene_dense, 'frame')  175 us
    all_gather x1, blocking collectives, per_device(): blocks = lax.all_gather(adapter_couple, 'frame', axis=0, tiled=True)  76 us
    all_gather x1, waiting for transfers between devices, per_device(): lax.all_gather(output_weight, 'fsdp', axis=0, tiled=True)  58.8 us
    all_to_all x1, waiting for transfers between devices, per_device(): lax.all_to_all(chosen.astype(jnp.bfloat16), 'fsdp', split_axis=0, concat_...  54 us
    all_to_all x1, blocking collectives, per_device(): lax.all_to_all(grad_terms, 'fsdp', split_axis=3, concat_axis=0, tiled=True)  42.7 us
    unnamed x1, blocking collectives  15.7 us
    unnamed x18, local copies, waits for them, and re-layouts  13 us
  transfers between devices with their start and end apart: 3, of which 3 were waited for; matrix products, arithmetic and copies ran while one was open for 3% of the time, Pallas kernels for 0%

commit v1 on v0

--- a/solution.py
+++ b/solution.py
@@ -108,7 +108,7 @@
     scene_dense = jnp.einsum(
         "fs,fxrd->sxrd", column_pick.astype(jnp.float32), pieces, precision=lax.Precision.HIGHEST
     )
-    scene_full = lax.psum(scene_dense, "frame")
+    scene_full = jnp.sum(lax.all_gather(scene_dense, "frame"), 0)
     owned_rows = lax.dynamic_slice_in_dim(scene_full, lax.axis_index("frame"), 1, 0)
     return (owned_rows[:, 0], owned_rows[:, 1], frame_loss)
 

time: 510 us -> 1030 us (2.02)
  waiting for transfers between devices: 289 us -> 801 us
  other arithmetic: 12.3 us -> 24 us
    all_gather x0 -> x1, waiting for transfers between devices: none -> 688 us  [per_device(): scene_full = jnp.sum(lax.all_gather(scene_dense, 'frame'), 0)]
    psum x1 -> x0, waiting for transfers between devices: 175 us -> none  [per_device(): scene_full = lax.psum(scene_dense, 'frame')]
    reduce_sum x0 -> x1, other arithmetic: none -> 13.1 us  [per_device(): scene_full = jnp.sum(lax.all_gather(scene_dense, 'frame'), 0)]
  transfers between devices with their start and end apart: 3 -> 3, of which waited for: 3 -> 3; matrix products, arithmetic and copies ran while one was open for 3% -> 2% of each run, Pallas kernels for 0% -> 0%
where the time goes in v1:
time: 1030 us
  waiting for transfers between devices  801 us (78%)
  blocking collectives  134 us (13%)
  local copies, waits for them, and re-layouts  27.5 us (3%)
  other arithmetic  24 us (2%)
  matrix products  22.5 us (2%)
  between operations  17.3 us (2%)
    all_gather x1, waiting for transfers between devices, per_device(): scene_full = jnp.sum(lax.all_gather(scene_dense, 'frame'), 0)  688 us
    all_gather x1, blocking collectives, per_device(): blocks = lax.all_gather(adapter_couple, 'frame', axis=0, tiled=True)  76 us
    all_gather x1, waiting for transfers between devices, per_device(): lax.all_gather(output_weight, 'fsdp', axis=0, tiled=True)  58.8 us
    all_to_all x1, waiting for transfers between devices, per_device(): lax.all_to_all(chosen.astype(jnp.bfloat16), 'fsdp', split_axis=0, concat_...  54 us
    all_to_all x1, blocking collectives, per_device(): lax.all_to_all(grad_terms, 'fsdp', split_axis=3, concat_axis=0, tiled=True)  42.7 us
  transfers between devices with their start and end apart: 3, of which 3 were waited for; matrix products, arithmetic and copies ran while one was open for 2% of the time, Pallas kernels for 0%

profile of v1, /device:TPU:16, one launch (start us, length us, event | category | flops | bytes accessed | tf_op | source)
XLA Modules:
  0.0 1031.9 jit_solution(17106012003785096691)
XLA Ops:
  7.2 0.0 all-gather.4.cloned.1.call-start
  7.2 0.7 all-gather.4.cloned.1.call-update
  8.6 1.3 dynamic-slice
  9.8 0.8 dynamic-update-slice
  10.6 15.7 %all-reduce = s32[16]{0:T(128)S(1)} all-reduce(s32[16]{0:T(128)S(1)} %dynamic-update-slice), channel_id=1, replica_groups=mesh['frame'=16,'fsdp'=16] {'fsdp'}, use_global_device_ids=true, to_apply=%add | all-reduce | flops 16 | bytes 128
  26.3 0.8 select_reduce_fusion
  27.1 0.8 pad_maximum_fusion.1
  27.9 76.0 %all_gather.17 = bf16[16,2,64,192]{3,2,1,0:T(8,128)(2,1)S(1)} all-gather(bf16[1,2,64,192]{3,2,1,0:T(8,128)(2,1)S(1)} %pad_maximum_fusion.1), channel_id=1, replica_groups=mesh['frame'=16,'fsdp'=16] {'frame'}, dimensions={0}, use_global_device_ids=true | all-gather | bytes 835584 | tf_op jit(solution)/shard_map/all_gather | solution.py:64
  103.9 0.7 convolution_convert_fusion
  104.6 0.0 copy-start
  104.6 1.3 copy.59
  106.0 4.8 all-to-all-start
  110.8 0.0 all-gather.6.cloned.1.call-start
  111.5 0.0 copy-done
  111.5 0.0 copy-start.1
  111.5 0.2 copy.70
  111.7 1.6 copy.71
  113.3 0.0 copy-done.1
  113.3 0.2 copy.72
  113.6 0.8 fusion.24
  114.4 2.0 fusion.51
  116.3 1.1 fusion.15
  117.5 1.8 copy.56
  119.3 54.0 %all-to-all-done = bf16[16,2,64,192]{3,2,1,0:T(8,128)(2,1)S(1)} async-done(((bf16[16,2,64,192]{3,2,1,0:T(8,128)(2,1)}), bf16[16,2,64,192]{3,2,1,0:T(8,128)(2,1)S(1)}, u32[]{:S(2)}, u32[]{:S(2)}) %all-to-all-start) | async-done | bytes 786464 | tf_op jit(solution)/shard_map/all_to_all | solution.py:71
  173.3 0.6 copy.60
  173.9 0.0 copy-start.2
  173.9 1.1 all_to_all.29
  175.0 1.8 fusion.33
  176.8 58.8 %all-gather.4.cloned.1.call-done = bf16[3072,3072]{1,0:T(8,128)(2,1)} async-done(((bf16[192,3072]{1,0:T(8,128)(2,1)}), bf16[3072,3072]{1,0:T(8,128)(2,1)}) %all-gather.4.cloned.1.call-update) | async-done | bytes 18874384 | tf_op jit(solution)/shard_map/all_gather | solution.py:55
  235.6 0.0 copy-done.2
  235.6 0.0 copy-start.3
  235.6 9.1 fusion.5
  244.7 0.0 copy-done.3
  244.7 1.5 multiply_reduce_fusion
  246.2 3.2 convolution_bitcast_fusion.1
  249.4 0.0 copy-start.4
  249.4 0.4 fusion.7
  249.7 0.7 copy-done.4
  250.5 1.3 pad_maximum_fusion
  251.7 4.4 copy.61
  256.2 4.2 reshape.121
  260.4 42.7 %all_to_all.36 = f32[16,1,24576]{2,1,0:T(1,128)S(1)} all-to-all(f32[16,1,24576]{2,1,0:T(1,128)} %reshape.121), channel_id=1, replica_groups=mesh['frame'=16,'fsdp'=16] {'fsdp'}, dimensions={0} | all-to-all | bytes 3145728 | tf_op jit(solution)/shard_map/all_to_all | solution.py:107
  303.1 0.5 broadcast.46
  303.7 6.0 reduce.5
  309.7 3.4 reshape.122
  313.1 3.8 copy.69
  316.9 4.0 fusion.12
  320.9 0.0 all-gather.6.cloned.1.call-update
  321.6 687.9 %all-gather.6.cloned.1.call-done = f32[256,2,64,192]{3,0,2,1:T(8,128)} async-done(((f32[16,2,64,192]{3,0,2,1:T(8,128)}), f32[256,2,64,192]{3,0,2,1:T(8,128)}) %all-gather.6.cloned.1.call-update) | async-done | bytes 25165840 | tf_op jit(solution)/shard_map/all_gather | solution.py:111
  1009.5 13.1 %reduce_sum.40 = f32[16,2,64,192]{3,0,2,1:T(8,128)S(1)} reduce(f32[16,16,2,64,192]{4,1,0,3,2:T(8,128)} %bitcast.98, f32[]{:T(128)} %constant.3.clone.1), dimensions={0}, to_apply=%region_3.4 | reduce | flops 5898240 | bytes 26738692 | tf_op jit(solution)/shard_map/reduce_sum | solution.py:111
  1022.6 0.1 dynamic-slice_bitcast_fusion
  1022.7 0.6 copy.64
  1023.3 0.6 copy.63
  (2 shorter events, 0.0 us)
Async XLA Ops:
  7.2 228.4 %all-gather.4.cloned.1.call-start = ((), (), s32[]{:S(2)}) async-start(), calls=%async_computation.2 | async-start | bytes 20054016 | tf_op jit(solution)/shard_map/all_gather | solution.py:55
  104.6 6.9 copy-start
  106.0 67.3 %all-to-all-start = ((bf16[16,2,64,192]{3,2,1,0:T(8,128)(2,1)}), bf16[16,2,64,192]{3,2,1,0:T(8,128)(2,1)S(1)}, u32[]{:S(2)}, u32[]{:S(2)}) async-start(bf16[16,2,64,192]{3,2,1,0:T(8,128)(2,1)} %copy.59), calls=%async_computation | async-start | bytes 2097152 | tf_op jit(solution)/shard_map/all_to_all | solution.py:71
  110.8 898.7 %all-gather.6.cloned.1.call-start = ((), (), s32[]{:S(2)}) async-start(), calls=%async_computation.3 | async-start | bytes 35651584 | tf_op jit(solution)/shard_map/all_gather | solution.py:111
  111.5 1.8 copy-start.1
  173.9 61.7 %copy-start.2 = (bf16[1,192,24,128]{3,2,1,0:T(8,128)(2,1)S(1)}, bf16[1,192,24,128]{3,2,1,0:T(8,128)(2,1)}, u32[]{:S(2)}) copy-start(bf16[1,192,24,128]{3,2,1,0:T(8,128)(2,1)} %copy.56) | copy-start | bytes 3538948
  235.6 9.1 copy-start.3
  249.4 1.1 copy-start.4
Sparse Core Ops, SparseCore 0:
  10.7 224.8 all-gather.3
  321.1 688.3 all-gather.5
